TPU v7x, 32 devices: a whole 2x2x4 slice. The times are simulated.
32 devices in a mesh: groups: 2 (over y), expert: 4 (over z), seq: 4 (over x, core).
Axes of the slice: x: 2, y: 2, z: 4, core: 2. Of those that a mesh axis runs over, the one named last changes fastest.
Arguments:
- inputs: bfloat16 [4096, 1024], P(('groups', 'expert', 'seq')), parts along dimension 0, may hold values from -6 to 6
- grad_out: bfloat16 [4096, 1024], P(('groups', 'expert', 'seq')), parts along dimension 0, may hold values from -4 to 4
- gates: bfloat16 [4096, 4], P(('groups', 'expert', 'seq')), parts along dimension 0, may hold values from 0.049804688 to 0.59765625
- expert_ids: int32 [4096, 4], P(('groups', 'expert', 'seq')), parts along dimension 0, may hold values from 0 to 3, as said below
- slot_index: int32 [4096, 4], P(('groups', 'expert', 'seq')), parts along dimension 0, may hold values from 0 to 127, as said below
- filter_taps: bfloat16 [256, 1024], replicated, may hold values from -0.375 to 0.375
- w_gate: bfloat16 [4, 1024, 512], P('expert', 'seq'), may hold values from -0.1875 to 0.1875
- w_up: bfloat16 [4, 1024, 512], P('expert', 'seq'), may hold values from -0.1875 to 0.1875
- w_down: bfloat16 [4, 512, 1024], P('expert', 'seq'), may hold values from -0.25 to 0.25
Outputs:
- grad_inputs: bfloat16 [4096, 1024], P(('groups', 'expert', 'seq')), parts along dimension 0
- grad_gates: bfloat16 [4096, 4], P(('groups', 'expert', 'seq')), parts along dimension 0
- grad_filter: float32 [512, 1024], P('groups'), parts along dimension 0
- grad_w_gate: bfloat16 [8, 1024, 512], P(('groups', 'expert'), 'seq'), parts along dimension 0
- grad_w_up: bfloat16 [8, 1024, 512], P(('groups', 'expert'), 'seq'), parts along dimension 0
- grad_w_down: bfloat16 [8, 512, 1024], P(('groups', 'expert'), 'seq'), parts along dimension 0
There are 2 independent parts, one for each index of `groups`. A program takes and returns all parts, laid end to end along the dimension named above; an argument that names none is the same for every part. Nothing has to cross between parts.
Inputs may be any that keep to these rules, and one draw needn't show every extreme that they name: `expert_ids`: each row names 4 different experts, and every expert is named by some row. Among the assignments of the 128 rows of one device that name the same expert, slot_index takes each of the values 0, 1, ... once, in an order of priority that is not row order; assignments with a slot of 128 or more are dropped.
All inputs are finite; a program needn't handle non-finite values.
Results may differ from a plain program's by a relative error of at most 0.009.
Values may be sent and summed in bfloat16 or wider, within the bound.
A program may use at most 64 MiB of HBM per device.

v0:
```python
import jax
import jax.numpy as jnp
from jax import lax
from jax.sharding import PartitionSpec as P


def from_behind(block, axis, distance):
    devices = range(lax.axis_size(axis))
    route = [(i - distance, i) for i in devices if i - distance in devices]
    return lax.ppermute(block, axis, route)


def depthwise(signal, kernel):
    return lax.conv_general_dilated(
        signal[None],
        kernel[:, None, :],
        (1,),
        "VALID",
        dimension_numbers=("NWC", "WIO", "NWC"),
        feature_group_count=signal.shape[1],
        preferred_element_type=jnp.float32,
    )[0]


def contract(left, right, left_dim, right_dim):
    return lax.dot_general(
        left, right, (((left_dim,), (right_dim,)), ((), ())), preferred_element_type=jnp.float32
    )


def expert_pass(token_rows, scaled_rows, gate_mat, up_mat, down_mat):
    pre_gate = jnp.dot(token_rows, gate_mat, preferred_element_type=jnp.float32)
    pre_up = jnp.dot(token_rows, up_mat, preferred_element_type=jnp.float32)
    sigma = jax.nn.sigmoid(pre_gate)
    swish = pre_gate * sigma
    hidden = (swish * pre_up).astype(jnp.bfloat16)
    outputs = jnp.dot(hidden, down_mat, preferred_element_type=jnp.float32).astype(jnp.bfloat16)
    grad_hidden = contract(scaled_rows, down_mat, 1, 1)
    grad_pre_gate = (grad_hidden * pre_up * (sigma * (1.0 + pre_gate * (1.0 - sigma)))).astype(
        jnp.bfloat16
    )
    grad_pre_up = (grad_hidden * swish).astype(jnp.bfloat16)
    part_gate = contract(token_rows, grad_pre_gate, 0, 0)
    part_up = contract(token_rows, grad_pre_up, 0, 0)
    part_down = contract(hidden, scaled_rows, 0, 0)
    grad_rows = (
        contract(grad_pre_gate, gate_mat, 1, 1) + contract(grad_pre_up, up_mat, 1, 1)
    ).astype(jnp.bfloat16)
    return (grad_rows, outputs, (part_gate, part_up, part_down))


def body(inputs, grad_out, gates, expert_ids, slot_index, filter_taps, w_gate, w_up, w_down):
    tok_count, width = inputs.shape
    taps = filter_taps.shape[0]
    top_count = expert_ids.shape[1]
    experts = lax.axis_size("expert")
    capacity = tok_count * top_count // experts
    reach = taps - 1
    shift_count = (reach + tok_count - 1) // tok_count
    earlier = [from_behind(inputs, "seq", shift_by) for shift_by in range(shift_count, 0, -1)]
    extended = jnp.concatenate(earlier + [inputs], axis=0)[-(tok_count + reach) :]
    filtered = depthwise(extended, filter_taps[::-1]).astype(jnp.bfloat16)
    kept = slot_index < capacity
    dest = jnp.where(kept, expert_ids * capacity + slot_index, experts * capacity).reshape(-1)

    def place(values):
        rest = values.shape[1:]
        empty = jnp.zeros((experts * capacity,) + rest, values.dtype)
        return empty.at[dest].set(values, mode="drop").reshape((experts, capacity) + rest)

    def fetch(buffer):
        rest = buffer.shape[2:]
        flat = buffer.reshape((experts * capacity,) + rest)
        return jnp.take(flat, dest, axis=0, mode="fill", fill_value=0).reshape(
            (tok_count, top_count) + rest
        )

    token_send = place(
        jnp.broadcast_to(filtered[:, None, :], (tok_count, top_count, width)).reshape(-1, width)
    )
    gate_full, up_full, down_full = (
        lax.all_gather(w_gate, "seq", axis=1, tiled=True),
        lax.all_gather(w_up, "seq", axis=1, tiled=True),
        lax.all_gather(w_down, "seq", axis=1, tiled=True),
    )
    gate_mat = gate_full[0]
    up_mat = up_full[0]
    down_mat = down_full[0]
    scaled = (
        gates.astype(jnp.float32)[:, :, None] * grad_out.astype(jnp.float32)[:, None, :]
    ).astype(jnp.bfloat16)
    token_recv, scaled_recv = (
        lax.all_to_all(token_send, "expert", split_axis=0, concat_axis=0, tiled=True),
        lax.all_to_all(
            place(scaled.reshape(-1, width)), "expert", split_axis=0, concat_axis=0, tiled=True
        ),
    )
    grad_rows, outputs, partials = expert_pass(
        token_recv.reshape(-1, width), scaled_recv.reshape(-1, width), gate_mat, up_mat, down_mat
    )
    grad_back, output_back = (
        lax.all_to_all(
            grad_rows.reshape(experts, capacity, width),
            "expert",
            split_axis=0,
            concat_axis=0,
            tiled=True,
        ),
        lax.all_to_all(
            outputs.reshape(experts, capacity, width),
            "expert",
            split_axis=0,
            concat_axis=0,
            tiled=True,
        ),
    )
    output_rows = fetch(output_back)
    grad_gates = jnp.sum(
        grad_out.astype(jnp.float32)[:, None, :] * output_rows.astype(jnp.float32), axis=2
    ).astype(jnp.bfloat16)
    summed_gate, summed_up, summed_down = (
        lax.psum_scatter(
            partials[0][None].astype(jnp.bfloat16), "seq", scatter_dimension=1, tiled=True
        ).astype(jnp.float32),
        lax.psum_scatter(
            partials[1][None].astype(jnp.bfloat16), "seq", scatter_dimension=1, tiled=True
        ).astype(jnp.float32),
        lax.psum_scatter(
            partials[2][None].astype(jnp.bfloat16), "seq", scatter_dimension=1, tiled=True
        ).astype(jnp.float32),
    )
    grad_filtered = jnp.sum(fetch(grad_back).astype(jnp.float32), axis=1).astype(jnp.bfloat16)
    later = [from_behind(grad_filtered, "seq", -shift_by) for shift_by in range(1, shift_count + 1)]
    grad_extended = jnp.concatenate([grad_filtered] + later, axis=0)[: tok_count + reach]
    grad_inputs = depthwise(grad_extended, filter_taps).astype(jnp.bfloat16)
    local_taps = depthwise(extended, grad_filtered)[::-1]
    grad_filter = lax.psum(local_taps, ("expert", "seq"))
    return (
        grad_inputs,
        grad_gates,
        grad_filter,
        summed_gate.astype(jnp.bfloat16),
        summed_up.astype(jnp.bfloat16),
        summed_down.astype(jnp.bfloat16),
    )


def solution(mesh):
    return jax.shard_map(
        body,
        mesh=mesh,
        in_specs=(
            P(("groups", "expert", "seq"), None),
            P(("groups", "expert", "seq"), None),
            P(("groups", "expert", "seq"), None),
            P(("groups", "expert", "seq"), None),
            P(("groups", "expert", "seq"), None),
            P(),
            P("expert", "seq", None),
            P("expert", "seq", None),
            P("expert", "seq", None),
        ),
        out_specs=(
            P(("groups", "expert", "seq"), None),
            P(("groups", "expert", "seq"), None),
            P("groups", None),
            P(("groups", "expert"), "seq", None),
            P(("groups", "expert"), "seq", None),
            P(("groups", "expert"), "seq", None),
        ),
        check_vma=False,
    )
```

profile of v0, /device:TPU:1, one launch (start us, length us, event | category | flops | bytes accessed | tf_op | source)
XLA Modules:
  0.0 351.8 jit_solution(16538734937356647307)
XLA Ops:
  7.9 4.7 %collective-permute-start = (bf16[128,1024]{1,0:T(8,128)(2,1)}, bf16[128,1024]{1,0:T(8,128)(2,1)}, u32[]{:S(2)}, u32[]{:S(2)}) collective-permute-start(bf16[128,1024]{1,0:T(8,128)(2,1)} %param.11), channel_id=1, source_target_pairs={{0,2},{1,3},{4,6},{5,7},{8,10},{9,11},{12,14},{13,15},{16,18},{17,... | collective-permute-start | bytes 786440 | tf_op jit(solution)/shard_map/ppermute | solution.py:10
  12.6 1.9 collective-permute-start.1
  15.4 0.8 copy.20
  16.3 2.8 mul.55
  19.2 2.0 mul.56
  21.2 3.6 %scatter_custom_fusion = bf16[512,1024]{1,0:T(8,128)(2,1)} fusion(s32[512]{0:T(512)S(1)} %bitcast.76, f32[512,1024]{1,0:T(8,128)S(1)} %mul.56, f32[512]{0:T(512)S(1)} %reshape.113, bf16[]{:T(256)} %constant.7.clone.1), kind=kCustom, calls=%fused_computation.21 | custom fusion | flops 1048576 | bytes 3147778 | tf_op jit(solution)/shard_map/scatter | solution.py:69
  24.8 4.7 %all-to-all-start = ((bf16[4,128,1024]{2,1,0:T(8,128)(2,1)}), bf16[4,128,1024]{2,1,0:T(8,128)(2,1)}, u32[]{:S(2)}, u32[]{:S(2)}) async-start(bf16[4,128,1024]{2,1,0:T(8,128)(2,1)} %bitcast.1), calls=%async_computation | async-start | bytes 2097152 | tf_op jit(solution)/shard_map/all_to_all | solution.py:94
  29.6 0.7 all-gather.8.cloned.1.call-update
  31.0 1.2 fusion.27
  32.3 14.0 %convolution_convert_fusion.4 = bf16[1,128,1024]{2,0,1:T(2,128)(2,1)S(1)} fusion(bf16[1,383,1024]{2,1,0:T(8,128)(2,1)S(1)} %fusion.27, bf16[256,1,1024]{2,0,1:T(8,128)(2,1)S(1)} %bitcast.74), kind=kOutput, calls=%fused_computation.17 | convolution fusion | flops 67239936 | bytes 1570816 | tf_op jit(solution)/shard_map/conv_general_dilated | solution.py:14
  46.6 1.1 reshape.142
  47.8 4.2 %scatter_custom_fusion.1 = bf16[512,1024]{1,0:T(8,128)(2,1)} fusion(s32[512]{0:T(512)S(1)} %bitcast.77, bf16[512,1024]{1,0:T(8,128)(2,1)} %reshape.142, bf16[]{:T(256)} %constant.7.clone.1), kind=kCustom, calls=%fused_computation.49 | custom fusion | bytes 1049088 | tf_op jit(solution)/shard_map/scatter | solution.py:69
  52.0 2.9 all-to-all-done
  54.9 3.5 all-to-all-start.1
  59.2 3.3 fusion.20
  62.4 21.2 %all-to-all-done.1 = bf16[4,128,1024]{2,1,0:T(8,128)(2,1)S(1)} async-done(((bf16[4,128,1024]{2,1,0:T(8,128)(2,1)}), bf16[4,128,1024]{2,1,0:T(8,128)(2,1)S(1)}, u32[]{:S(2)}, u32[]{:S(2)}) %all-to-all-start.1) | async-done | bytes 1048608 | tf_op jit(solution)/shard_map/all_to_all | solution.py:93
  83.6 1.0 copy-done.1
  84.6 2.9 fusion.14
  87.5 4.1 %multiply_convert_fusion.2 = (bf16[512,512]{1,0:T(8,128)(2,1)}, bf16[512,512]{1,0:T(8,128)(2,1)S(1)}, bf16[512,512]{1,0:T(8,128)(2,1)S(1)}) fusion(f32[512,512]{1,0:T(8,128)} %fusion.14, f32[512,512]{1,0:T(8,128)} %fusion.20, bf16[512,1024]{1,0:T(8,128)(2,1)} %bitcast.68, bf16[1,1024,512]{2,1,0:T(8,128)(2,1)} %all-gather.6.cloned.1.call-done), kind=kOutput, calls=%fused_computation.35 | convolution fusion | flops 540803072 | bytes 5767168 | tf_op jit(solution)/shard_map/dot_general | solution.py:33
  91.6 0.7 fusion.12
  92.4 0.8 copy-done.3
  93.2 1.7 add_convert_fusion
  94.9 3.5 all-to-all-start.2
  98.6 25.0 %all-to-all-done.2 = bf16[4,128,1024]{2,1,0:T(8,128)(2,1)S(1)} async-done(((bf16[4,128,1024]{2,1,0:T(8,128)(2,1)}), bf16[4,128,1024]{2,1,0:T(8,128)(2,1)S(1)}, u32[]{:S(2)}, u32[]{:S(2)}) %all-to-all-start.2) | async-done | bytes 1048608 | tf_op jit(solution)/shard_map/all_to_all | solution.py:102
  123.6 2.8 gather_fusion
  126.4 1.4 broadcast_select_fusion
  127.8 1.2 reshape.110
  129.0 2.5 reduce_sum.21
  131.5 15.1 %fusion.8 = f32[1,256,1024]{2,0,1:T(1,128)S(1)} fusion(bf16[1,383,1024]{2,1,0:T(8,128)(2,1)} %copy-done.4, bf16[128,1,1024]{2,0,1:T(8,128)(2,1)S(1)} %bitcast.72), kind=kOutput, calls=%fused_computation.18 | convolution fusion | flops 67108864 | bytes 2095104 | tf_op jit(solution)/shard_map/conv_general_dilated | solution.py:14
  146.8 5.3 %rev.7 = f32[256,1024]{1,0:T(8,128)} reverse(f32[256,1024]{1,0:T(8,128)S(1)} %bitcast.64), dimensions={0} | reverse | bytes 2097152 | tf_op jit(solution)/shard_map/rev | solution.py:136
  152.2 3.2 fusion.4
  155.4 2.8 fusion.3
  158.3 3.1 convolution_convert_fusion.3
  161.3 3.5 %all-to-all-start.3 = ((bf16[4,128,1024]{2,1,0:T(8,128)(2,1)}), bf16[4,128,1024]{2,1,0:T(8,128)(2,1)S(1)}, u32[]{:S(2)}, u32[]{:S(2)}) async-start(bf16[4,128,1024]{2,1,0:T(8,128)(2,1)} %bitcast.71), calls=%async_computation.3 | async-start | bytes 2097152 | tf_op jit(solution)/shard_map/all_to_all | solution.py:109
  164.9 1.3 collective-permute-start.3
  166.2 3.6 %collective-permute-start.2 = (bf16[128,1024]{1,0:T(8,128)(2,1)S(1)}, bf16[128,1024]{1,0:T(8,128)(2,1)}, u32[]{:S(2)}, u32[]{:S(2)}) collective-permute-start(bf16[128,1024]{1,0:T(8,128)(2,1)S(1)} %reduce_sum.21), channel_id=1, source_target_pairs={{1,0},{2,1},{3,2},{5,4},{6,5},{7,6},{9,8},{10,9},{11,10},{13,12},{... | collective-permute-start | bytes 786440 | tf_op jit(solution)/shard_map/ppermute | solution.py:10
  169.8 3.1 fusion.2
  172.9 20.6 %all-to-all-done.3 = bf16[4,128,1024]{2,1,0:T(8,128)(2,1)S(1)} async-done(((bf16[4,128,1024]{2,1,0:T(8,128)(2,1)}), bf16[4,128,1024]{2,1,0:T(8,128)(2,1)S(1)}, u32[]{:S(2)}, u32[]{:S(2)}) %all-to-all-start.3) | async-done | bytes 1048608 | tf_op jit(solution)/shard_map/all_to_all | solution.py:109
  193.5 2.8 gather_fusion.1
  196.3 1.7 multiply_reduce_fusion
  198.8 1.1 fusion.26
  199.9 14.0 %fusion.5 = bf16[1,128,1024]{2,0,1:T(2,128)(2,1)S(1)} fusion(bf16[1,383,1024]{2,1,0:T(8,128)(2,1)S(1)} %fusion.26, bf16[256,1,1024]{2,0,1:T(8,128)(2,1)S(1)} %bitcast.73), kind=kOutput, calls=%fused_computation.16 | convolution fusion | flops 67239936 | bytes 1570816 | tf_op jit(solution)/shard_map/conv_general_dilated | solution.py:14
  213.9 0.8 copy.49
  214.6 44.2 %all-reduce.2.cloned.1.call-done = f32[256,1024]{1,0:T(8,128)} async-done(((f32[256,1024]{1,0:T(8,128)}), f32[256,1024]{1,0:T(8,128)}) %all-reduce.2.cloned.1.call-update) | async-done | bytes 1048592 | tf_op jit(solution)/shard_map/psum | solution.py:137
  258.9 27.7 %reduce-scatter.8.cloned.1.call-done = bf16[1,128,1024]{2,1,0:T(8,128)(2,1)} async-done(((bf16[1,512,1024]{2,1,0:T(8,128)(2,1)}), bf16[1,128,1024]{2,1,0:T(8,128)(2,1)}) %reduce-scatter.8.cloned.1.call-update) | async-done | bytes 262160 | tf_op jit(solution)/shard_map/reduce_scatter | solution.py:128
  286.6 28.0 %reduce-scatter.6.cloned.1.call-done = bf16[1,256,512]{2,1,0:T(8,128)(2,1)} async-done(((bf16[1,1024,512]{2,1,0:T(8,128)(2,1)}), bf16[1,256,512]{2,1,0:T(8,128)(2,1)}) %reduce-scatter.6.cloned.1.call-update) | async-done | bytes 262160 | tf_op jit(solution)/shard_map/reduce_scatter | solution.py:125
  314.6 28.0 %reduce-scatter.4.cloned.1.call-done = bf16[1,256,512]{2,1,0:T(8,128)(2,1)} async-done(((bf16[1,1024,512]{2,1,0:T(8,128)(2,1)}), bf16[1,256,512]{2,1,0:T(8,128)(2,1)}) %reduce-scatter.4.cloned.1.call-update) | async-done | bytes 262160 | tf_op jit(solution)/shard_map/reduce_scatter | solution.py:122
  342.7 2.3 copy.52
  (53 shorter events, 5.0 us)
Async XLA Ops:
  7.2 52.0 %all-gather.4.cloned.1.call-start = ((), (), s32[]{:S(2)}) async-start(), calls=%async_computation.7 | async-start | bytes 1310720 | tf_op jit(solution)/shard_map/all_gather | solution.py:84
  7.9 23.1 %collective-permute-start = (bf16[128,1024]{1,0:T(8,128)(2,1)}, bf16[128,1024]{1,0:T(8,128)(2,1)}, u32[]{:S(2)}, u32[]{:S(2)}) collective-permute-start(bf16[128,1024]{1,0:T(8,128)(2,1)} %param.11), channel_id=1, source_target_pairs={{0,2},{1,3},{4,6},{5,7},{8,10},{9,11},{12,14},{13,15},{16,18},{17,... | collective-permute-start | bytes 786440 | tf_op jit(solution)/shard_map/ppermute | solution.py:10
  12.6 18.4 %collective-permute-start.1 = (bf16[128,1024]{1,0:T(8,128)(2,1)}, bf16[128,1024]{1,0:T(8,128)(2,1)}, u32[]{:S(2)}, u32[]{:S(2)}) collective-permute-start(bf16[128,1024]{1,0:T(8,128)(2,1)} %param.11), channel_id=1, source_target_pairs={{0,1},{1,2},{2,3},{4,5},{5,6},{6,7},{8,9},{9,10},{10,11},{12,13},{... | collective-permute-start | bytes 786440 | tf_op jit(solution)/shard_map/ppermute | solution.py:10
  21.2 9.1 %copy-start.7 = (bf16[256,1024]{1,0:T(8,128)(2,1)S(1)}, bf16[256,1024]{1,0:T(8,128)(2,1)}, u32[]{:S(2)}) copy-start(bf16[256,1024]{1,0:T(8,128)(2,1)} %param.16) | copy-start | bytes 1572868
  24.8 6.2 %copy-start.9 = (bf16[128,1024]{1,0:T(8,128)(2,1)S(1)}, bf16[128,1024]{1,0:T(8,128)(2,1)}, u32[]{:S(2)}) copy-start(bf16[128,1024]{1,0:T(8,128)(2,1)} %param.11) | copy-start | bytes 786436
  24.8 30.0 %all-to-all-start = ((bf16[4,128,1024]{2,1,0:T(8,128)(2,1)}), bf16[4,128,1024]{2,1,0:T(8,128)(2,1)}, u32[]{:S(2)}, u32[]{:S(2)}) async-start(bf16[4,128,1024]{2,1,0:T(8,128)(2,1)} %bitcast.1), calls=%async_computation | async-start | bytes 2097152 | tf_op jit(solution)/shard_map/all_to_all | solution.py:94
  29.6 32.9 %all-gather.8.cloned.1.call-start = ((), (), s32[]{:S(2)}) async-start(), calls=%async_computation.9 | async-start | bytes 1310720 | tf_op jit(solution)/shard_map/all_gather | solution.py:82
  32.2 14.0 %copy-start.4 = (bf16[1,383,1024]{2,1,0:T(8,128)(2,1)}, bf16[1,383,1024]{2,1,0:T(8,128)(2,1)S(1)}, u32[]{:S(2)}) copy-start(bf16[1,383,1024]{2,1,0:T(8,128)(2,1)S(1)} %fusion.27) | copy-start | bytes 2353156
  54.9 28.7 %all-to-all-start.1 = ((bf16[4,128,1024]{2,1,0:T(8,128)(2,1)}), bf16[4,128,1024]{2,1,0:T(8,128)(2,1)S(1)}, u32[]{:S(2)}, u32[]{:S(2)}) async-start(bf16[4,128,1024]{2,1,0:T(8,128)(2,1)} %bitcast.6), calls=%async_computation.1 | async-start | bytes 2097152 | tf_op jit(solution)/shard_map/all_to_all | solution.py:93
  58.4 29.1 %all-gather.6.cloned.1.call-start = ((), (), s32[]{:S(2)}) async-start(), calls=%async_computation.8 | async-start | bytes 1310720 | tf_op jit(solution)/shard_map/all_gather | solution.py:83
  83.6 1.0 copy-start.1
  87.5 4.1 %copy-start = (bf16[1,1024,512]{2,1,0:T(8,128)(2,1)S(1)}, bf16[1,1024,512]{2,1,0:T(8,128)(2,1)}, u32[]{:S(2)}) copy-start(bf16[1,1024,512]{2,1,0:T(8,128)(2,1)} %all-gather.8.cloned.1.call-done) | copy-start | bytes 3145732
  91.6 0.8 copy-start.5
  91.6 3.3 copy-start.6
  91.6 1.6 copy-start.3
  94.9 28.7 %all-to-all-start.2 = ((bf16[4,128,1024]{2,1,0:T(8,128)(2,1)}), bf16[4,128,1024]{2,1,0:T(8,128)(2,1)S(1)}, u32[]{:S(2)}, u32[]{:S(2)}) async-start(bf16[4,128,1024]{2,1,0:T(8,128)(2,1)} %bitcast.65), calls=%async_computation.2 | async-start | bytes 2097152 | tf_op jit(solution)/shard_map/all_to_all | solution.py:102
  98.4 160.4 %all-reduce.2.cloned.1.call-start = ((), (), s32[]{:S(2)}) async-start(), calls=%async_computation.10 | async-start | bytes 2097152 | tf_op jit(solution)/shard_map/psum | solution.py:137
  152.1 3.3 copy-start.2
  152.1 134.5 %reduce-scatter.8.cloned.1.call-start = ((), (), s32[]{:S(2)}) async-start(), calls=%async_computation.13 | async-start | bytes 1310720 | tf_op jit(solution)/shard_map/reduce_scatter | solution.py:128
  155.4 159.2 %reduce-scatter.6.cloned.1.call-start = ((), (), s32[]{:S(2)}) async-start(), calls=%async_computation.12 | async-start | bytes 1310720 | tf_op jit(solution)/shard_map/reduce_scatter | solution.py:125
  161.3 32.2 %all-to-all-start.3 = ((bf16[4,128,1024]{2,1,0:T(8,128)(2,1)}), bf16[4,128,1024]{2,1,0:T(8,128)(2,1)S(1)}, u32[]{:S(2)}, u32[]{:S(2)}) async-start(bf16[4,128,1024]{2,1,0:T(8,128)(2,1)} %bitcast.71), calls=%async_computation.3 | async-start | bytes 2097152 | tf_op jit(solution)/shard_map/all_to_all | solution.py:109
  164.9 177.8 %reduce-scatter.4.cloned.1.call-start = ((), (), s32[]{:S(2)}) async-start(), calls=%async_computation.11 | async-start | bytes 1310720 | tf_op jit(solution)/shard_map/reduce_scatter | solution.py:122
  164.9 33.9 %collective-permute-start.3 = (bf16[128,1024]{1,0:T(8,128)(2,1)S(1)}, bf16[128,1024]{1,0:T(8,128)(2,1)}, u32[]{:S(2)}, u32[]{:S(2)}) collective-permute-start(bf16[128,1024]{1,0:T(8,128)(2,1)S(1)} %reduce_sum.21), channel_id=1, source_target_pairs={{2,0},{3,1},{6,4},{7,5},{10,8},{11,9},{14,12},{15,13},{18,16},{19,... | collective-permute-start | bytes 786440 | tf_op jit(solution)/shard_map/ppermute | solution.py:10
  166.2 32.6 %collective-permute-start.2 = (bf16[128,1024]{1,0:T(8,128)(2,1)S(1)}, bf16[128,1024]{1,0:T(8,128)(2,1)}, u32[]{:S(2)}, u32[]{:S(2)}) collective-permute-start(bf16[128,1024]{1,0:T(8,128)(2,1)S(1)} %reduce_sum.21), channel_id=1, source_target_pairs={{1,0},{2,1},{3,2},{5,4},{6,5},{7,6},{9,8},{10,9},{11,10},{13,12},{... | collective-permute-start | bytes 786440 | tf_op jit(solution)/shard_map/ppermute | solution.py:10
  196.3 3.6 %copy-start.8 = (bf16[256,1024]{1,0:T(8,128)(2,1)S(1)}, bf16[256,1024]{1,0:T(8,128)(2,1)}, u32[]{:S(2)}) copy-start(bf16[256,1024]{1,0:T(8,128)(2,1)} %param.16) | copy-start | bytes 1572868
Sparse Core Ops, SparseCore 0:
  9.6 19.1 all-gather.3
  31.9 18.4 all-gather.7
  60.8 18.3 all-gather.5
  152.2 106.5 all-reduce.1
  261.8 24.7 reduce-scatter.7
  289.7 24.8 reduce-scatter.5
  317.7 24.8 reduce-scatter.3
where the time goes:
time: 353 us; the launch traced here: 352 us
  waiting for transfers between devices  200 us (57%)
  matrix products  67.9 us (19%)
  local copies, waits for them, and re-layouts  30.5 us (9%)
  starting transfers between devices  27.2 us (8%)
  between operations  14.4 us (4%)
  other arithmetic  12.2 us (3%)
    psum x1, waiting for transfers between devices, body(): grad_filter = lax.psum(local_taps, ('expert', 'seq'))  44.2 us
    conv_general_dilated x3, matrix products, depthwise(): lax.conv_general_dilated(signal[None], kernel[:, None, :], (1,), 'VALID',...  43 us
    reduce_scatter x1, waiting for transfers between devices, body(): lax.psum_scatter(partials[1][None].astype(jnp.bfloat16), 'seq', scatter_d...  28 us
    reduce_scatter x1, waiting for transfers between devices, body(): lax.psum_scatter(partials[0][None].astype(jnp.bfloat16), 'seq', scatter_d...  28 us
    reduce_scatter x1, waiting for transfers between devices, body(): lax.psum_scatter(partials[2][None].astype(jnp.bfloat16), 'seq', scatter_d...  27.7 us
    all_to_all x1, waiting for transfers between devices, body(): lax.all_to_all(grad_rows.reshape(experts, capacity, width), 'expert', spl...  25 us
    all_to_all x1, waiting for transfers between devices, body(): lax.all_to_all(token_send, 'expert', split_axis=0, concat_axis=0, tiled=T...  21.2 us
    all_to_all x1, waiting for transfers between devices, body(): lax.all_to_all(outputs.reshape(experts, capacity, width), 'expert', split...  20.6 us
  transfers between devices with their start and end apart: 15, of which 8 were waited for; matrix products, arithmetic and copies ran while one was open for 20% of the time, Pallas kernels for 0%

commit v1 on v0

--- a/solution.py
+++ b/solution.py
@@ -1,7 +1,16 @@
+import functools
+
 import jax
 import jax.numpy as jnp
+import numpy as np
 from jax import lax
+from jax.experimental import pallas as pl
+from jax.experimental.pallas import tpu as pltpu
 from jax.sharding import PartitionSpec as P
+
+MESH = pl.DeviceIdType.MESH
+F32 = jnp.float32
+BF16 = jnp.bfloat16
 
 
 def from_behind(block, axis, distance):
@@ -49,7 +58,7 @@
     return (grad_rows, outputs, (part_gate, part_up, part_down))
 
 
-def body(inputs, grad_out, gates, expert_ids, slot_index, filter_taps, w_gate, w_up, w_down):
+def routed_body(inputs, grad_out, gates, expert_ids, slot_index, filter_taps, w_gate, w_up, w_down):
     tok_count, width = inputs.shape
     taps = filter_taps.shape[0]
     top_count = expert_ids.shape[1]
@@ -145,9 +154,369 @@
     )
 
 
+def transforms(size):
+    freq = 2.0 * np.pi * (np.arange(size // 2) + 0.5) / size
+    angle = freq[:, None] * np.arange(size)[None, :]
+    forward = np.concatenate([np.cos(angle), np.sin(angle)], axis=0)
+    inverse = forward.T * (2.0 / size)
+
+    def pieces(matrix):
+        high = matrix.astype(jnp.bfloat16)
+        low = (matrix - high.astype(np.float64)).astype(jnp.bfloat16)
+        return high, low
+
+    return pieces(forward) + pieces(inverse)
+
+
+def mm(left, right):
+    return jnp.dot(left, right, preferred_element_type=F32)
+
+
+def dense_kernel(
+    rows_ref, cot_ref, pack_ref, taps_ref, fh_ref, fl_ref, ih_ref, il_ref,
+    gin_ref, gg_ref, gf_ref, gw_ref,
+    xext, tap_spec, x_spec, tall, gall, wall, hid, gpre, scaled, back, rall,
+    part, sib_in, pair, cross_in, gext, gfs, gf_in, gfz, gfz_in, gfo, gfull,
+    send_sem, recv_sem,
+):
+    z = lax.axis_index("expert")
+    q = lax.axis_index("seq")
+    tok, width = rows_ref.shape
+    size = xext.shape[0]
+    half = size // 2
+    reach_at = size - tok
+    dq = 2 * tok
+    ff = hid.shape[1]
+    fq = ff // 4
+    chunk = 256
+    chunks = width // chunk
+    sib = q + 1 - 2 * (q % 2)
+    cross = (q + 2) % 4
+    far = (sib + 2) % 4
+
+    def link(n, src, dst, axis, peer):
+        return pltpu.make_async_remote_copy(
+            src_ref=src, dst_ref=dst, send_sem=send_sem.at[n], recv_sem=recv_sem.at[n],
+            device_id={axis: peer}, device_id_type=MESH,
+        )
+
+    barrier = pltpu.get_barrier_semaphore()
+    for s in range(1, 4):
+        pl.semaphore_signal(barrier, inc=1, device_id={"expert": (z + s) % 4}, device_id_type=MESH)
+        pl.semaphore_signal(barrier, inc=1, device_id={"seq": (q + s) % 4}, device_id_type=MESH)
+    pl.semaphore_wait(barrier, 6)
+
+    halo = [
+        link(n, rows_ref, xext.at[pl.ds(reach_at - (n + 1) * tok, tok)], "seq", (q + n + 1) % 4)
+        for n in range(2)
+    ]
+    for n in range(2):
+        @pl.when(q + n + 1 < 4)
+        def _(n=n):
+            halo[n].start()
+
+        @pl.when(q < n + 1)
+        def _(n=n):
+            xext[pl.ds(reach_at - (n + 1) * tok, tok)] = jnp.zeros((tok, width), BF16)
+
+    cots = [link(1 + s, cot_ref, gall.at[s], "expert", (z + s) % 4) for s in range(1, 4)]
+    for copy in cots:
+        copy.start()
+    w_sib = link(8, pack_ref, wall.at[q], "seq", sib)
+    w_cross = link(9, pack_ref, wall.at[q], "seq", cross)
+    w_sib.start()
+    w_cross.start()
+    wall[q] = pack_ref[...]
+    gall[0] = cot_ref[...]
+    xext[pl.ds(reach_at, tok)] = rows_ref[...]
+
+    def cols(c):
+        return pl.ds(pl.multiple_of(c * chunk, chunk), chunk)
+
+    def forward(first, count, values):
+        span = slice(first, first + count)
+        return mm(fh_ref[:, span], values) + mm(fl_ref[:, span], values)
+
+    def backward(first, count, spec):
+        span = slice(first, first + count)
+        high = spec.astype(BF16)
+        low = (spec - high.astype(F32)).astype(BF16)
+        return mm(ih_ref[span], high) + mm(il_ref[span], high) + mm(ih_ref[span], low)
+
+    taps = taps_ref.shape[0]
+
+    @pl.loop(0, chunks)
+    def _(c):
+        tap_spec[:, cols(c)] = forward(0, taps, taps_ref[:, cols(c)])
+
+    for n in range(2):
+        @pl.when(q >= n + 1)
+        def _(n=n):
+            halo[n].wait_recv()
+
+    @pl.loop(0, chunks)
+    def _(c):
+        spec = forward(0, size, xext[:, cols(c)])
+        x_spec[:, cols(c)] = spec
+        xc, xs = spec[:half], spec[half:]
+        hc, hs = tap_spec[:half, cols(c)], tap_spec[half:, cols(c)]
+        prod = jnp.concatenate([xc * hc - xs * hs, xc * hs + xs * hc], axis=0)
+        tall[0, :, cols(c)] = backward(reach_at, tok, prod).astype(BF16)
+
+    rows_out = [link(4 + s, tall.at[0], tall.at[s], "expert", (z + s) % 4) for s in range(1, 4)]
+    for copy in rows_out:
+        copy.start()
+
+    w_cross.wait_recv()
+    w_far = link(10, wall.at[cross], wall.at[cross], "seq", sib)
+    w_far.start()
+    w_sib.wait_recv()
+    w_far.wait_recv()
+
+    def turned(left, right):
+        return lax.dot_general(left, right, (((1,), (1,)), ((), ())), preferred_element_type=F32)
+
+    lanes = lax.broadcasted_iota(jnp.int32, (tok, 128), 1)
+    backs = [
+        link(10 + s, back.at[s], rall.at[s], "expert", (z + 4 - s) % 4) for s in range(1, 4)
+    ]
+    for s in range(4):
+        if s:
+            cots[s - 1].wait_recv()
+            rows_out[s - 1].wait_recv()
+        span = pl.ds(s * tok, tok)
+        pre = mm(tall[s, :, 0:dq], wall[0, :dq, :])
+        for k in range(1, 4):
+            pre += mm(tall[s, :, k * dq:(k + 1) * dq], wall[k, :dq, :])
+        cot = gall[s, :, :width]
+        weight = jnp.sum(
+            jnp.where(lanes == z, gall[s, :, width:].astype(F32), 0.0), axis=1, keepdims=True
+        )
+        raw = jnp.concatenate([turned(cot, wall[k, dq:, :]) for k in range(4)], axis=1)
+        gate, up = pre[:, :ff], pre[:, ff:]
+        sigma = jax.nn.sigmoid(gate)
+        swish = gate * sigma
+        hidden = (swish * up).astype(BF16)
+        gg = jnp.sum(hidden.astype(F32) * raw, axis=1, keepdims=True)
+        grad_hidden = raw * weight
+        grad_gate = grad_hidden * up * (sigma * (1.0 + gate * (1.0 - sigma)))
+        gp = jnp.concatenate([grad_gate.astype(BF16), (grad_hidden * swish).astype(BF16)], axis=1)
+        hid[span] = hidden
+        gpre[span] = gp
+        scaled[span] = (weight * cot.astype(F32)).astype(BF16)
+        target = back if s else rall
+        for k in range(4):
+            target[s, :, k * dq:(k + 1) * dq] = turned(gp, wall[k, :dq, :]).astype(BF16)
+        target[s, :, width:] = jnp.broadcast_to(gg, (tok, 128)).astype(BF16)
+        if s:
+            backs[s - 1].start()
+
+    def across(left, right):
+        return lax.dot_general(left, right, (((0,), (0,)), ((), ())), preferred_element_type=F32)
+
+    def partial(slot, dest):
+        top = jnp.zeros((dq, 2 * ff), F32)
+        low = jnp.zeros((fq, width), F32)
+        wide = pl.ds(pl.multiple_of(dest * dq, dq), dq)
+        thin = pl.ds(pl.multiple_of(dest * fq, fq), fq)
+        for s in range(4):
+            top += across(tall[s, :, wide], gpre[pl.ds(s * tok, tok)])
+        low = across(hid[:, thin], scaled[...])
+        part[slot, :dq] = top.astype(BF16)
+        part[slot, dq:] = low.astype(BF16)
+
+    to_sib = [link(14 + n, part.at[n], sib_in.at[n], "seq", sib) for n in range(2)]
+    partial(0, far)
+    to_sib[0].start()
+    partial(1, sib)
+    to_sib[1].start()
+    partial(2, cross)
+
+    for copy in backs:
+        copy.wait_recv()
+    total = jnp.zeros((tok, width), F32)
+    gates_all = jnp.zeros((tok, 128), F32)
+    for s in range(4):
+        total += rall[s, :, :width].astype(F32)
+        gates_all += jnp.where(lanes == (z + s) % 4, rall[s, :, width:].astype(F32), 0.0)
+    gg_ref[...] = gates_all
+    gext[pl.ds(0, tok)] = total.astype(BF16)
+    halo_back = [
+        link(17 + n, gext.at[pl.ds(0, tok)], gext.at[pl.ds((n + 1) * tok, tok)], "seq", (q + 3 - n) % 4)
+        for n in range(2)
+    ]
+    for n in range(2):
+        @pl.when(q >= n + 1)
+        def _(n=n):
+            halo_back[n].start()
+
+        @pl.when(q + n + 1 >= 4)
+        def _(n=n):
+            gext[pl.ds((n + 1) * tok, tok)] = jnp.zeros((tok, width), BF16)
+
+    to_sib[0].wait_recv()
+    pair[...] = (part[2].astype(F32) + sib_in[0].astype(F32)).astype(BF16)
+    to_cross = link(16, pair, cross_in, "seq", cross)
+
+    quarter = taps // 4
+
+    @pl.loop(0, chunks)
+    def _(c):
+        spec = forward(reach_at, tok, gext[pl.ds(0, tok), cols(c)])
+        gc, gs = spec[:half], spec[half:]
+        xc, xs = x_spec[:half, cols(c)], x_spec[half:, cols(c)]
+        prod = jnp.concatenate([gc * xc + gs * xs, gs * xc - gc * xs], axis=0)
+        result = backward(0, taps, prod).astype(BF16)
+        for k in range(4):
+            gfs[k, :, cols(c)] = result[k * quarter:(k + 1) * quarter]
+
+    gf_seq = [
+        link(18 + s, gfs.at[(q + s) % 4], gf_in.at[s], "seq", (q + s) % 4) for s in range(1, 4)
+    ]
+    for copy in gf_seq:
+        copy.start()
+    to_cross.start()
+    partial(3, q)
+
+    for copy in gf_seq:
+        copy.wait_recv()
+    mine = gfs[q].astype(F32)
+    for s in range(1, 4):
+        mine += gf_in[s].astype(F32)
+    piece = quarter // 4
+    for k in range(4):
+        gfz[k] = mine[k * piece:(k + 1) * piece].astype(BF16)
+    gf_exp = [
+        link(21 + s, gfz.at[(z + s) % 4], gfz_in.at[s], "expert", (z + s) % 4) for s in range(1, 4)
+    ]
+    for copy in gf_exp:
+        copy.start()
+
+    for n in range(2):
+        @pl.when(q + n + 1 < 4)
+        def _(n=n):
+            halo_back[n].wait_recv()
+
+    for copy in gf_exp:
+        copy.wait_recv()
+    mine = gfz[z].astype(F32)
+    for s in range(1, 4):
+        mine += gfz_in[s].astype(F32)
+    gfull[q, z] = mine.astype(BF16)
+    gf_out = [
+        link(24 + s, gfull.at[q, z], gfull.at[q, z], "expert", (z + s) % 4) for s in range(1, 4)
+    ]
+    for copy in gf_out:
+        copy.start()
+
+    @pl.loop(0, chunks)
+    def _(c):
+        spec = forward(0, size, gext[:, cols(c)])
+        gc, gs = spec[:half], spec[half:]
+        hc, hs = tap_spec[:half, cols(c)], tap_spec[half:, cols(c)]
+        prod = jnp.concatenate([gc * hc + gs * hs, gs * hc - gc * hs], axis=0)
+        gin_ref[:, cols(c)] = backward(0, tok, prod).astype(BF16)
+
+    for copy in gf_out:
+        copy.wait_recv()
+    gf_last = [link(27 + s, gfull.at[q], gfull.at[q], "seq", (q + s) % 4) for s in range(1, 4)]
+    for copy in gf_last:
+        copy.start()
+
+    to_sib[1].wait_recv()
+    to_cross.wait_recv()
+    gw_ref[...] = (
+        part[3].astype(F32) + sib_in[1].astype(F32) + cross_in[...].astype(F32)
+    ).astype(BF16)
+
+    for copy in gf_last:
+        copy.wait_recv()
+    for a in range(4):
+        for b in range(4):
+            gf_ref[pl.ds((a * 4 + b) * piece, piece)] = gfull[a, b].astype(F32)
+
+    for n in range(2):
+        @pl.when(q + n + 1 < 4)
+        def _(n=n):
+            halo[n].wait_send()
+
+        @pl.when(q >= n + 1)
+        def _(n=n):
+            halo_back[n].wait_send()
+    for copy in (
+        cots + [w_sib, w_cross, w_far] + rows_out + backs + to_sib + [to_cross]
+        + gf_seq + gf_exp + gf_out + gf_last
+    ):
+        copy.wait_send()
+
+
+def dense_body(inputs, grad_out, gates, expert_ids, slot_index, filter_taps, w_gate, w_up, w_down):
+    tok, width = inputs.shape
+    taps = filter_taps.shape[0]
+    ff = w_gate.shape[2]
+    experts = expert_ids.shape[1]
+    size = taps + tok
+    kept = slot_index < tok
+    named = (expert_ids[:, :, None] == jnp.arange(experts)[None, None, :]) & kept[:, :, None]
+    by_expert = jnp.sum(jnp.where(named, gates.astype(F32)[:, :, None], 0.0), axis=1).astype(BF16)
+    cot = jnp.concatenate([grad_out, jnp.pad(by_expert, ((0, 0), (0, 128 - experts)))], axis=1)
+    pack = jnp.concatenate([jnp.concatenate([w_gate[0], w_up[0]], axis=1), w_down[0]], axis=0)
+    rows = pack.shape[0]
+    ext = width + 128
+    vm = lambda *shape: pltpu.VMEM(shape, BF16)
+    grad_inputs, gate_grads, grad_filter, weights = pl.pallas_call(
+        dense_kernel,
+        out_shape=(
+            jax.ShapeDtypeStruct((tok, width), BF16),
+            jax.ShapeDtypeStruct((tok, 128), F32),
+            jax.ShapeDtypeStruct((taps, width), F32),
+            jax.ShapeDtypeStruct((rows, width), BF16),
+        ),
+        in_specs=[pl.BlockSpec(memory_space=pltpu.VMEM)] * 8,
+        out_specs=(pl.BlockSpec(memory_space=pltpu.VMEM),) * 4,
+        scratch_shapes=[
+            vm(size, width), pltpu.VMEM((size, width), F32), pltpu.VMEM((size, width), F32),
+            vm(4, tok, width), vm(4, tok, ext), vm(4, rows, width),
+            vm(4 * tok, ff), vm(4 * tok, 2 * ff), vm(4 * tok, width),
+            vm(4, tok, ext), vm(4, tok, ext),
+            vm(4, rows, width), vm(2, rows, width), vm(rows, width), vm(rows, width),
+            vm(size, width), vm(4, taps // 4, width), vm(4, taps // 4, width),
+            vm(4, taps // 16, width), vm(4, taps // 16, width), vm(8, 128),
+            vm(4, 4, taps // 16, width),
+            pltpu.SemaphoreType.DMA((32,)), pltpu.SemaphoreType.DMA((32,)),
+        ],
+        compiler_params=pltpu.CompilerParams(
+            collective_id=0, has_side_effects=True, vmem_limit_bytes=52 * 1024 * 1024
+        ),
+    )(inputs, cot, pack, filter_taps, *[jnp.asarray(m) for m in transforms(size)])
+    picked = jnp.where(named, gate_grads[:, None, :experts], 0.0)
+    grad_gates = jnp.sum(picked, axis=2).astype(BF16)
+    dq = w_gate.shape[1]
+    return (
+        grad_inputs,
+        grad_gates,
+        grad_filter,
+        weights[None, :dq, :ff],
+        weights[None, :dq, ff:],
+        weights[None, dq:, :],
+    )
+
+
+def body_of(mesh):
+    def body(*args):
+        top_count = args[3].shape[1]
+        tok, taps, dq = args[0].shape[0], args[5].shape[0], args[6].shape[1]
+        small = mesh.shape["expert"] == top_count == 4 and mesh.shape["seq"] == 4
+        if small and taps == 2 * tok and dq == 2 * tok and 2 * args[6].shape[2] == args[0].shape[1]:
+            return dense_body(*args)
+        return routed_body(*args)
+
+    return body
+
+
 def solution(mesh):
     return jax.shard_map(
-        body,
+        body_of(mesh),
         mesh=mesh,
         in_specs=(
             P(("groups", "expert", "seq"), None),

time: 353 us -> 140 us (0.40)
  waiting for transfers between devices: 200 us -> 0 us
  Pallas kernels: 0 us -> 128 us
  matrix products: 67.9 us -> 0 us
  starting transfers between devices: 27.2 us -> 0 us
  local copies, waits for them, and re-layouts: 30.5 us -> 5.51 us
  between operations: 14.4 us -> 0.69 us
  other arithmetic: 12.2 us -> 5.8 us
    pallas_call x0 -> x1, Pallas kernels: none -> 128 us  [dense_body(): pl.pallas_call(dense_kernel, out_shape=(jax.ShapeDtypeStruct((tok, width)...]
    reduce_scatter x3 -> x0, waiting for transfers between devices: 83.8 us -> none  [the longest x1 28 us: body(): lax.psum_scatter(partials[1][None].astype(jnp.bfloat16), 'seq', scatter_d...]
    all_to_all x4 -> x0, waiting for transfers between devices: 69.6 us -> none  [the longest x1 25 us: body(): lax.all_to_all(grad_rows.reshape(experts, capacity, width), 'expert', spl...]
    psum x1 -> x0, waiting for transfers between devices: 44.2 us -> none  [body(): grad_filter = lax.psum(local_taps, ('expert', 'seq'))]
    conv_general_dilated x3 -> x0, matrix products: 43 us -> none  [depthwise(): lax.conv_general_dilated(signal[None], kernel[:, None, :], (1,), 'VALID',...]
    dot_general x9 -> x0, matrix products: 24.9 us -> none  [the longest x6 14.8 us: contract(): lax.dot_general(left, right, (((left_dim,), (right_dim,)), ((), ())), pre...]
    all_to_all x4 -> x0, starting transfers between devices: 15.3 us -> none  [the longest x1 4.7 us: body(): lax.all_to_all(place(scaled.reshape(-1, width)), 'expert', split_axis=0,...]
    ppermute x4 -> x0, starting transfers between devices: 11.5 us -> none  [from_behind(): return lax.ppermute(block, axis, route)]
  transfers between devices with their start and end apart: 15 -> 0, of which waited for: 8 -> 0; matrix products, arithmetic and copies ran while one was open for 20% -> 0% of each run, Pallas kernels for 0% -> 0%
where the time goes in v1:
time: 140 us
  Pallas kernels  128 us (91%)
  other arithmetic  5.8 us (4%)
  local copies, waits for them, and re-layouts  5.51 us (4%)
    pallas_call x1, Pallas kernels, dense_body(): pl.pallas_call(dense_kernel, out_shape=(jax.ShapeDtypeStruct((tok, width)...  128 us

profile of v1, /device:TPU:1, one launch (start us, length us, event | category | flops | bytes accessed | tf_op | source)
XLA Modules:
  0.0 140.0 jit_solution(4001594071010776105)
XLA Ops:
  0.6 0.7 broadcast_compare_fusion
  1.3 0.7 convert_element_type.11
  2.0 0.7 select_reduce_fusion.1
  2.7 0.1 copy.24
  2.8 0.0 copy-start
  2.8 0.0 copy-start.1
  2.9 0.0 copy-start.2
  2.9 0.0 copy-start.3
  2.9 1.1 fusion.1.cot_ref
  3.9 2.1 %pad_maximum_fusion.pack_ref = bf16[384,1024]{1,0:T(8,128)(2,1)} fusion(bf16[128,1024]{1,0:T(8,128)(2,1)} %bitcast.11, bf16[256,512]{1,0:T(8,128)(2,1)} %bitcast.12, bf16[256,512]{1,0:T(8,128)(2,1)} %bitcast.13), kind=kLoop, calls=%fused_computation | loop fusion | flops 2359296 | bytes 1572864 | tf_op jit(solution)/shard_map/concatenate | solution.py:463
  6.0 0.0 copy-done
  6.0 0.0 copy-done.1
  6.0 0.0 copy-done.2
  6.0 0.0 copy-done.3
  6.0 0.0 copy-start.5
  6.0 128.0 %shard_map.172 = (bf16[128,1024]{1,0:T(8,128)(2,1)S(1)}, f32[128,128]{1,0:T(8,128)S(1)}, f32[256,1024]{1,0:T(8,128)}, bf16[384,1024]{1,0:T(8,128)(2,1)}) custom-call(bf16[128,1024]{1,0:T(8,128)(2,1)S(1)} %copy-done.3, bf16[128,1152]{1,0:T(8,128)(2,1)S(1)} %fusion.1.cot_ref, bf16[384,1024]{1,0:T(8,128)(2,1)} %pad_maximum_fusion.pack_ref, ...), custom_call_target="tpu_custom_call" | custom-call | tf_op jit(solution)/shard_map/pallas_call | solution.py:467
  134.0 0.1 copy.25
  134.1 0.0 copy-done.5
  134.1 0.6 select_reduce_fusion
  134.7 0.0 copy-start.4
  134.7 1.8 %slice_bitcast_fusion = bf16[1,128,1024]{2,1,0:T(8,128)(2,1)} fusion(bf16[384,1024]{1,0:T(8,128)(2,1)} %get-tuple-element.13), kind=kLoop, calls=%fused_computation.4 | loop fusion | bytes 524288 | tf_op jit(solution)/shard_map/broadcast_in_dim | solution.py:501
  136.5 1.9 %slice_bitcast_fusion.1 = (bf16[1,256,512]{2,1,0:T(8,128)(2,1)}, bf16[1,256,512]{2,1,0:T(8,128)(2,1)}) fusion(bf16[384,1024]{1,0:T(8,128)(2,1)} %get-tuple-element.13), kind=kLoop, calls=%fused_computation.5 | loop fusion | bytes 1048576 | tf_op jit(solution)/shard_map/broadcast_in_dim | solution.py:500
  138.3 0.7 copy.28
  139.0 0.0 copy-done.4
  139.0 1.0 copy.29
Async XLA Ops:
  2.8 3.2 %copy-start = (bf16[384,384]{1,0:T(8,128)(2,1)S(1)}, bf16[384,384]{1,0:T(8,128)(2,1)}, u32[]{:S(2)}) copy-start(bf16[384,384]{1,0:T(8,128)(2,1)} %constant.17.clone.ih_ref) | copy-start | bytes 884740
  2.8 3.2 %copy-start.1 = (bf16[384,384]{1,0:T(8,128)(2,1)S(1)}, bf16[384,384]{1,0:T(8,128)(2,1)}, u32[]{:S(2)}) copy-start(bf16[384,384]{1,0:T(8,128)(2,1)} %constant.16.clone.fl_ref) | copy-start | bytes 884740
  2.9 3.2 %copy-start.2 = (bf16[384,384]{1,0:T(8,128)(2,1)S(1)}, bf16[384,384]{1,0:T(8,128)(2,1)}, u32[]{:S(2)}) copy-start(bf16[384,384]{1,0:T(8,128)(2,1)} %constant.15.clone.fh_ref) | copy-start | bytes 884740
  2.9 3.2 %copy-start.3 = (bf16[128,1024]{1,0:T(8,128)(2,1)S(1)}, bf16[128,1024]{1,0:T(8,128)(2,1)}, u32[]{:S(2)}) copy-start(bf16[128,1024]{1,0:T(8,128)(2,1)} %rows_ref.1) | copy-start | bytes 786436
  6.0 128.1 %copy-start.5 = (s32[128,4]{0,1:T(4,128)S(1)}, s32[128,4]{0,1:T(4,128)}, u32[]{:S(2)}) copy-start(s32[128,4]{0,1:T(4,128)} %param.16) | copy-start | bytes 6148
  134.7 4.3 %copy-start.4 = (f32[256,1024]{1,0:T(8,128)S(1)}, f32[256,1024]{1,0:T(8,128)}, u32[]{:S(2)}) copy-start(f32[256,1024]{1,0:T(8,128)} %get-tuple-element.24) | copy-start | bytes 3145732

commit v2 on v1

--- a/solution.py
+++ b/solution.py
@@ -173,10 +173,12 @@
 
 
 def dense_kernel(
-    rows_ref, cot_ref, pack_ref, taps_ref, fh_ref, fl_ref, ih_ref, il_ref,
-    gin_ref, gg_ref, gf_ref, gw_ref,
+    rows_ref, cot_ref, gates_ref, ids_ref, slots_ref, wg_ref, wu_ref, wd_ref, taps_ref,
+    fh_ref, fl_ref, ih_ref, il_ref,
+    gin_ref, gg_ref, gf_ref, dg_ref, du_ref, dd_ref,
     xext, tap_spec, x_spec, tall, gall, wall, hid, gpre, scaled, back, rall,
-    part, sib_in, pair, cross_in, gext, gfs, gf_in, gfz, gfz_in, gfo, gfull,
+    part, sib_in, pair, cross_in, gext, gfs, gf_in, gfz, gfz_in, gfull,
+    weigh, sums, sums_in,
     send_sem, recv_sem,
 ):
     z = lax.axis_index("expert")
@@ -219,14 +221,35 @@
         def _(n=n):
             xext[pl.ds(reach_at - (n + 1) * tok, tok)] = jnp.zeros((tok, width), BF16)
 
+    ids = ids_ref[...]
+    held = jnp.where(slots_ref[...] < tok, gates_ref[...].astype(F32), 0.0)
+    eye = lax.broadcasted_iota(jnp.int32, (tok, tok), 0) == lax.broadcasted_iota(
+        jnp.int32, (tok, tok), 1
+    )
+
+    def as_row(column):
+        return jnp.sum(jnp.where(eye, column, 0.0), axis=0, keepdims=True)
+
+    def as_column(row):
+        return jnp.sum(jnp.where(eye, row, 0.0), axis=1, keepdims=True)
+
+    weigh[0] = jnp.zeros(weigh.shape[1:], F32)
+    for e in range(4):
+        weigh[0, e:e + 1] = as_row(
+            jnp.sum(jnp.where(ids == e, held, 0.0), axis=1, keepdims=True)
+        )
+    weighs = [link(30 + s, weigh.at[0], weigh.at[s], "expert", (z + s) % 4) for s in range(1, 4)]
+    for copy in weighs:
+        copy.start()
     cots = [link(1 + s, cot_ref, gall.at[s], "expert", (z + s) % 4) for s in range(1, 4)]
     for copy in cots:
         copy.start()
-    w_sib = link(8, pack_ref, wall.at[q], "seq", sib)
-    w_cross = link(9, pack_ref, wall.at[q], "seq", cross)
+    wall[q, :dq, :ff] = wg_ref[0]
+    wall[q, :dq, ff:] = wu_ref[0]
+    wall[q, dq:] = wd_ref[0]
+    w_sib = link(8, wall.at[q], wall.at[q], "seq", sib)
+    w_cross = link(9, wall.at[q], wall.at[q], "seq", cross)
     w_sib.start()
-    w_cross.start()
-    wall[q] = pack_ref[...]
     gall[0] = cot_ref[...]
     xext[pl.ds(reach_at, tok)] = rows_ref[...]
 
@@ -253,6 +276,8 @@
         @pl.when(q >= n + 1)
         def _(n=n):
             halo[n].wait_recv()
+
+    w_cross.start()
 
     @pl.loop(0, chunks)
     def _(c):
@@ -276,21 +301,25 @@
     def turned(left, right):
         return lax.dot_general(left, right, (((1,), (1,)), ((), ())), preferred_element_type=F32)
 
-    lanes = lax.broadcasted_iota(jnp.int32, (tok, 128), 1)
+    sublanes = lax.broadcasted_iota(jnp.int32, weigh.shape[1:], 0)
+    gate_sums = [
+        link(33 + s, sums.at[s], sums_in.at[s], "expert", (z + 4 - s) % 4) for s in range(1, 4)
+    ]
     backs = [
         link(10 + s, back.at[s], rall.at[s], "expert", (z + 4 - s) % 4) for s in range(1, 4)
     ]
     for s in range(4):
         if s:
+            weighs[s - 1].wait_recv()
             cots[s - 1].wait_recv()
             rows_out[s - 1].wait_recv()
         span = pl.ds(s * tok, tok)
         pre = mm(tall[s, :, 0:dq], wall[0, :dq, :])
         for k in range(1, 4):
             pre += mm(tall[s, :, k * dq:(k + 1) * dq], wall[k, :dq, :])
-        cot = gall[s, :, :width]
-        weight = jnp.sum(
-            jnp.where(lanes == z, gall[s, :, width:].astype(F32), 0.0), axis=1, keepdims=True
+        cot = gall[s]
+        weight = as_column(
+            jnp.sum(jnp.where(sublanes == z, weigh[s], 0.0), axis=0, keepdims=True)
         )
         raw = jnp.concatenate([turned(cot, wall[k, dq:, :]) for k in range(4)], axis=1)
         gate, up = pre[:, :ff], pre[:, ff:]
@@ -307,8 +336,9 @@
         target = back if s else rall
         for k in range(4):
             target[s, :, k * dq:(k + 1) * dq] = turned(gp, wall[k, :dq, :]).astype(BF16)
-        target[s, :, width:] = jnp.broadcast_to(gg, (tok, 128)).astype(BF16)
+        (sums if s else sums_in)[s] = jnp.broadcast_to(as_row(gg), sums.shape[1:])
         if s:
+            gate_sums[s - 1].start()
             backs[s - 1].start()
 
     def across(left, right):
@@ -331,15 +361,17 @@
     partial(1, sib)
     to_sib[1].start()
     partial(2, cross)
+    to_sib[0].wait_recv()
+    pair[...] = (part[2].astype(F32) + sib_in[0].astype(F32)).astype(BF16)
+    to_cross = link(16, pair, cross_in, "seq", cross)
+    to_cross.start()
+    partial(3, q)
 
     for copy in backs:
         copy.wait_recv()
     total = jnp.zeros((tok, width), F32)
-    gates_all = jnp.zeros((tok, 128), F32)
     for s in range(4):
-        total += rall[s, :, :width].astype(F32)
-        gates_all += jnp.where(lanes == (z + s) % 4, rall[s, :, width:].astype(F32), 0.0)
-    gg_ref[...] = gates_all
+        total += rall[s].astype(F32)
     gext[pl.ds(0, tok)] = total.astype(BF16)
     halo_back = [
         link(17 + n, gext.at[pl.ds(0, tok)], gext.at[pl.ds((n + 1) * tok, tok)], "seq", (q + 3 - n) % 4)
@@ -354,9 +386,12 @@
         def _(n=n):
             gext[pl.ds((n + 1) * tok, tok)] = jnp.zeros((tok, width), BF16)
 
-    to_sib[0].wait_recv()
-    pair[...] = (part[2].astype(F32) + sib_in[0].astype(F32)).astype(BF16)
-    to_cross = link(16, pair, cross_in, "seq", cross)
+    for copy in gate_sums:
+        copy.wait_recv()
+    gate_grads = jnp.zeros(ids.shape, F32)
+    for s in range(4):
+        gate_grads += jnp.where(ids == (z + s) % 4, as_column(sums_in[s, 0:1]), 0.0)
+    gg_ref[...] = jnp.where(slots_ref[...] < tok, gate_grads, 0.0).astype(BF16)
 
     quarter = taps // 4
 
@@ -375,8 +410,6 @@
     ]
     for copy in gf_seq:
         copy.start()
-    to_cross.start()
-    partial(3, q)
 
     for copy in gf_seq:
         copy.wait_recv()
@@ -425,9 +458,12 @@
 
     to_sib[1].wait_recv()
     to_cross.wait_recv()
-    gw_ref[...] = (
+    weights = (
         part[3].astype(F32) + sib_in[1].astype(F32) + cross_in[...].astype(F32)
     ).astype(BF16)
+    dg_ref[0] = weights[:dq, :ff]
+    du_ref[0] = weights[:dq, ff:]
+    dd_ref[0] = weights[dq:]
 
     for copy in gf_last:
         copy.wait_recv()
@@ -444,7 +480,7 @@
         def _(n=n):
             halo_back[n].wait_send()
     for copy in (
-        cots + [w_sib, w_cross, w_far] + rows_out + backs + to_sib + [to_cross]
+        weighs + gate_sums + cots + [w_sib, w_cross, w_far] + rows_out + backs + to_sib + [to_cross]
         + gf_seq + gf_exp + gf_out + gf_last
     ):
         copy.wait_send()
@@ -454,51 +490,39 @@
     tok, width = inputs.shape
     taps = filter_taps.shape[0]
     ff = w_gate.shape[2]
-    experts = expert_ids.shape[1]
     size = taps + tok
-    kept = slot_index < tok
-    named = (expert_ids[:, :, None] == jnp.arange(experts)[None, None, :]) & kept[:, :, None]
-    by_expert = jnp.sum(jnp.where(named, gates.astype(F32)[:, :, None], 0.0), axis=1).astype(BF16)
-    cot = jnp.concatenate([grad_out, jnp.pad(by_expert, ((0, 0), (0, 128 - experts)))], axis=1)
-    pack = jnp.concatenate([jnp.concatenate([w_gate[0], w_up[0]], axis=1), w_down[0]], axis=0)
-    rows = pack.shape[0]
-    ext = width + 128
+    rows = w_gate.shape[1] + w_down.shape[1]
     vm = lambda *shape: pltpu.VMEM(shape, BF16)
-    grad_inputs, gate_grads, grad_filter, weights = pl.pallas_call(
+    return pl.pallas_call(
         dense_kernel,
         out_shape=(
             jax.ShapeDtypeStruct((tok, width), BF16),
-            jax.ShapeDtypeStruct((tok, 128), F32),
+            jax.ShapeDtypeStruct(gates.shape, BF16),
             jax.ShapeDtypeStruct((taps, width), F32),
-            jax.ShapeDtypeStruct((rows, width), BF16),
-        ),
-        in_specs=[pl.BlockSpec(memory_space=pltpu.VMEM)] * 8,
-        out_specs=(pl.BlockSpec(memory_space=pltpu.VMEM),) * 4,
+            jax.ShapeDtypeStruct(w_gate.shape, BF16),
+            jax.ShapeDtypeStruct(w_up.shape, BF16),
+            jax.ShapeDtypeStruct(w_down.shape, BF16),
+        ),
+        in_specs=[pl.BlockSpec(memory_space=pltpu.VMEM)] * 13,
+        out_specs=(pl.BlockSpec(memory_space=pltpu.VMEM),) * 6,
         scratch_shapes=[
             vm(size, width), pltpu.VMEM((size, width), F32), pltpu.VMEM((size, width), F32),
-            vm(4, tok, width), vm(4, tok, ext), vm(4, rows, width),
+            vm(4, tok, width), vm(4, tok, width), vm(4, rows, width),
             vm(4 * tok, ff), vm(4 * tok, 2 * ff), vm(4 * tok, width),
-            vm(4, tok, ext), vm(4, tok, ext),
+            vm(4, tok, width), vm(4, tok, width),
             vm(4, rows, width), vm(2, rows, width), vm(rows, width), vm(rows, width),
             vm(size, width), vm(4, taps // 4, width), vm(4, taps // 4, width),
-            vm(4, taps // 16, width), vm(4, taps // 16, width), vm(8, 128),
+            vm(4, taps // 16, width), vm(4, taps // 16, width),
             vm(4, 4, taps // 16, width),
-            pltpu.SemaphoreType.DMA((32,)), pltpu.SemaphoreType.DMA((32,)),
+            pltpu.VMEM((4, 8, tok), F32), pltpu.VMEM((4, 8, tok), F32), pltpu.VMEM((4, 8, tok), F32),
+            pltpu.SemaphoreType.DMA((37,)), pltpu.SemaphoreType.DMA((37,)),
         ],
         compiler_params=pltpu.CompilerParams(
             collective_id=0, has_side_effects=True, vmem_limit_bytes=52 * 1024 * 1024
         ),
-    )(inputs, cot, pack, filter_taps, *[jnp.asarray(m) for m in transforms(size)])
-    picked = jnp.where(named, gate_grads[:, None, :experts], 0.0)
-    grad_gates = jnp.sum(picked, axis=2).astype(BF16)
-    dq = w_gate.shape[1]
-    return (
-        grad_inputs,
-        grad_gates,
-        grad_filter,
-        weights[None, :dq, :ff],
-        weights[None, :dq, ff:],
-        weights[None, dq:, :],
+    )(
+        inputs, grad_out, gates, expert_ids, slot_index, w_gate, w_up, w_down, filter_taps,
+        *[jnp.asarray(m) for m in transforms(size)],
     )
 
 
@@ -507,7 +531,7 @@
         top_count = args[3].shape[1]
         tok, taps, dq = args[0].shape[0], args[5].shape[0], args[6].shape[1]
         small = mesh.shape["expert"] == top_count == 4 and mesh.shape["seq"] == 4
-        if small and taps == 2 * tok and dq == 2 * tok and 2 * args[6].shape[2] == args[0].shape[1]:
+        if small and tok == 128 and taps == 2 * tok and dq == 2 * tok and 2 * args[6].shape[2] == args[0].shape[1]:
             return dense_body(*args)
         return routed_body(*args)
 

time: 140 us -> 132 us (0.943)
  Pallas kernels: 128 us -> 120 us
  other arithmetic: 5.8 us -> 0 us
  local copies, waits for them, and re-layouts: 5.51 us -> 10.2 us
    pallas_call x1, Pallas kernels: 128 us -> 120 us  [dense_body(): pl.pallas_call(dense_kernel, out_shape=(jax.ShapeDtypeStruct((tok, width)...]
    unnamed x14 -> x18, local copies, waits for them, and re-layouts: 1.71 us -> 9.57 us
    broadcast_in_dim x2 -> x0, local copies, waits for them, and re-layouts: 3.61 us -> none  [the longest x1 1.85 us: dense_body(): weights[None, :dq, ff:]]
    concatenate x2 -> x0, other arithmetic: 3.13 us -> none  [the longest x1 2.06 us: dense_body(): jnp.concatenate([jnp.concatenate([w_gate[0], w_up[0]], axis=1), w_down[0]...]
where the time goes in v2:
time: 132 us; the launch traced here: 131 us
  Pallas kernels  120 us (91%)
  local copies, waits for them, and re-layouts  10.2 us (8%)
    pallas_call x1, Pallas kernels, dense_body(): pl.pallas_call(dense_kernel, out_shape=(jax.ShapeDtypeStruct((tok, width)...  120 us
    unnamed x18, local copies, waits for them, and re-layouts  9.57 us

profile of v2, /device:TPU:1, one launch (start us, length us, event | category | flops | bytes accessed | tf_op | source)
XLA Modules:
  0.0 130.8 jit_solution(7814639247005534136)
XLA Ops:
  0.6 0.0 copy-start.3
  0.6 0.8 copy.19.gates_ref
  1.5 0.0 copy-done.3
  1.5 0.0 copy-start.4
  1.5 0.1 copy.20.ids_ref
  1.6 0.6 copy-done.4
  2.1 0.1 copy.21.slots_ref
  2.3 0.0 copy-start
  2.3 0.9 copy-done
  3.2 0.0 copy-start.1
  3.2 0.9 copy-done.1
  4.2 0.0 copy-start.2
  4.2 0.9 copy-done.2
  5.1 119.9 %shard_map.172 = (bf16[128,1024]{1,0:T(8,128)(2,1)S(1)}, bf16[128,4]{1,0:T(8,128)(2,1)S(1)}, f32[256,1024]{1,0:T(8,128)}, bf16[1,256,512]{2,1,0:T(8,128)(2,1)S(1...) custom-call(bf16[128,1024]{1,0:T(8,128)(2,1)S(1)} %copy-done, bf16[128,1024]{1,0:T(8,128)(2,1)S(1)} %copy-done.1, ...), custom_call_target="tpu_custom_call" | custom-call | tf_op jit(solution)/shard_map/pallas_call | solution.py:496
  125.0 0.7 copy.22
  125.7 0.7 copy.28
  126.4 2.3 %copy.29 = f32[256,1024]{1,0:T(8,128)} copy(f32[256,1024]{1,0:T(8,128)} %get-tuple-element.20) | data formatting | bytes 2097152
  128.7 0.7 copy.30
  129.4 0.7 copy.31
  130.1 0.7 copy.32
Async XLA Ops:
  0.6 0.8 copy-start.3
  1.5 0.7 copy-start.4
  2.3 0.9 copy-start
  3.2 0.9 copy-start.1
  4.2 0.9 copy-start.2

commit v3 on v2

--- a/solution.py
+++ b/solution.py
@@ -196,11 +196,39 @@
     cross = (q + 2) % 4
     far = (sib + 2) % 4
 
-    def link(n, src, dst, axis, peer):
+    def link(n, src, dst, axis, peer, arrival=None):
         return pltpu.make_async_remote_copy(
-            src_ref=src, dst_ref=dst, send_sem=send_sem.at[n], recv_sem=recv_sem.at[n],
+            src_ref=src, dst_ref=dst, send_sem=send_sem.at[n],
+            recv_sem=recv_sem.at[n if arrival is None else arrival],
             device_id={axis: peer}, device_id_type=MESH,
         )
+
+    def pick(a, b, c, d):
+        return jnp.where(z == 0, a, jnp.where(z == 1, b, jnp.where(z == 2, c, d)))
+
+    def hop(base, buf, origin, step):
+        return link(
+            base + (0 if step > 0 else 4) + origin, buf.at[origin], buf.at[origin],
+            "expert", (z + 4 + step) % 4, base + origin,
+        )
+
+    def spread(base, buf, distance, send=True):
+        for step in (1, -1):
+            origin = z - step * distance
+            has_origin = origin >= 0 if step > 0 else origin <= 3
+            has_next = z < 3 if step > 0 else z > 0
+
+            @pl.when(has_origin)
+            def _(origin=origin, has_next=has_next, step=step):
+                if distance and send:
+                    hop(base, buf, origin, step).wait_recv()
+
+                @pl.when(has_next)
+                def _():
+                    if send:
+                        hop(base, buf, origin, step).start()
+                    else:
+                        hop(base, buf, origin, step).wait_send()
 
     barrier = pltpu.get_barrier_semaphore()
     for s in range(1, 4):
@@ -233,24 +261,24 @@
     def as_column(row):
         return jnp.sum(jnp.where(eye, row, 0.0), axis=1, keepdims=True)
 
-    weigh[0] = jnp.zeros(weigh.shape[1:], F32)
+    weigh[z] = jnp.zeros(weigh.shape[1:], F32)
     for e in range(4):
-        weigh[0, e:e + 1] = as_row(
+        weigh[z, e:e + 1] = as_row(
             jnp.sum(jnp.where(ids == e, held, 0.0), axis=1, keepdims=True)
         )
-    weighs = [link(30 + s, weigh.at[0], weigh.at[s], "expert", (z + s) % 4) for s in range(1, 4)]
+    weighs = [
+        link(30 + s, weigh.at[z], weigh.at[z], "expert", (z + s) % 4, 61 + z) for s in range(1, 4)
+    ]
     for copy in weighs:
         copy.start()
-    cots = [link(1 + s, cot_ref, gall.at[s], "expert", (z + s) % 4) for s in range(1, 4)]
-    for copy in cots:
-        copy.start()
+    gall[z] = cot_ref[...]
+    spread(37, gall, 0)
     wall[q, :dq, :ff] = wg_ref[0]
     wall[q, :dq, ff:] = wu_ref[0]
     wall[q, dq:] = wd_ref[0]
     w_sib = link(8, wall.at[q], wall.at[q], "seq", sib)
     w_cross = link(9, wall.at[q], wall.at[q], "seq", cross)
     w_sib.start()
-    gall[0] = cot_ref[...]
     xext[pl.ds(reach_at, tok)] = rows_ref[...]
 
     def cols(c):
@@ -272,6 +300,7 @@
     def _(c):
         tap_spec[:, cols(c)] = forward(0, taps, taps_ref[:, cols(c)])
 
+    spread(37, gall, 1)
     for n in range(2):
         @pl.when(q >= n + 1)
         def _(n=n):
@@ -286,11 +315,11 @@
         xc, xs = spec[:half], spec[half:]
         hc, hs = tap_spec[:half, cols(c)], tap_spec[half:, cols(c)]
         prod = jnp.concatenate([xc * hc - xs * hs, xc * hs + xs * hc], axis=0)
-        tall[0, :, cols(c)] = backward(reach_at, tok, prod).astype(BF16)
-
-    rows_out = [link(4 + s, tall.at[0], tall.at[s], "expert", (z + s) % 4) for s in range(1, 4)]
-    for copy in rows_out:
-        copy.start()
+        tall[z, :, cols(c)] = backward(reach_at, tok, prod).astype(BF16)
+
+    spread(45, tall, 0)
+    spread(37, gall, 2)
+    spread(45, tall, 1)
 
     w_cross.wait_recv()
     w_far = link(10, wall.at[cross], wall.at[cross], "seq", sib)
@@ -301,25 +330,31 @@
     def turned(left, right):
         return lax.dot_general(left, right, (((1,), (1,)), ((), ())), preferred_element_type=F32)
 
+    origins = [z, pick(1, 0, 1, 2), pick(2, 2, 3, 1), pick(3, 3, 0, 0)]
     sublanes = lax.broadcasted_iota(jnp.int32, weigh.shape[1:], 0)
     gate_sums = [
-        link(33 + s, sums.at[s], sums_in.at[s], "expert", (z + 4 - s) % 4) for s in range(1, 4)
+        link(33 + s, sums.at[s], sums_in.at[z], "expert", origins[s], 57 + z)
+        for s in range(1, 4)
     ]
     backs = [
-        link(10 + s, back.at[s], rall.at[s], "expert", (z + 4 - s) % 4) for s in range(1, 4)
+        link(10 + s, back.at[s], rall.at[z], "expert", origins[s], 53 + z) for s in range(1, 4)
     ]
     for s in range(4):
-        if s:
-            weighs[s - 1].wait_recv()
-            cots[s - 1].wait_recv()
-            rows_out[s - 1].wait_recv()
+        origin = origins[s]
+        if s == 1:
+            spread(37, gall, 3)
+            for k in range(1, 4):
+                peer = (z + k) % 4
+                link(30 + k, weigh.at[peer], weigh.at[peer], "expert", peer, 61 + peer).wait_recv()
+        elif s > 1:
+            spread(45, tall, s)
         span = pl.ds(s * tok, tok)
-        pre = mm(tall[s, :, 0:dq], wall[0, :dq, :])
+        pre = mm(tall[origin, :, 0:dq], wall[0, :dq, :])
         for k in range(1, 4):
-            pre += mm(tall[s, :, k * dq:(k + 1) * dq], wall[k, :dq, :])
-        cot = gall[s]
+            pre += mm(tall[origin, :, k * dq:(k + 1) * dq], wall[k, :dq, :])
+        cot = gall[origin]
         weight = as_column(
-            jnp.sum(jnp.where(sublanes == z, weigh[s], 0.0), axis=0, keepdims=True)
+            jnp.sum(jnp.where(sublanes == z, weigh[origin], 0.0), axis=0, keepdims=True)
         )
         raw = jnp.concatenate([turned(cot, wall[k, dq:, :]) for k in range(4)], axis=1)
         gate, up = pre[:, :ff], pre[:, ff:]
@@ -333,10 +368,10 @@
         hid[span] = hidden
         gpre[span] = gp
         scaled[span] = (weight * cot.astype(F32)).astype(BF16)
-        target = back if s else rall
+        target, at = (back, s) if s else (rall, z)
         for k in range(4):
-            target[s, :, k * dq:(k + 1) * dq] = turned(gp, wall[k, :dq, :]).astype(BF16)
-        (sums if s else sums_in)[s] = jnp.broadcast_to(as_row(gg), sums.shape[1:])
+            target[at, :, k * dq:(k + 1) * dq] = turned(gp, wall[k, :dq, :]).astype(BF16)
+        (sums if s else sums_in)[at] = jnp.broadcast_to(as_row(gg), sums.shape[1:])
         if s:
             gate_sums[s - 1].start()
             backs[s - 1].start()
@@ -350,7 +385,7 @@
         wide = pl.ds(pl.multiple_of(dest * dq, dq), dq)
         thin = pl.ds(pl.multiple_of(dest * fq, fq), fq)
         for s in range(4):
-            top += across(tall[s, :, wide], gpre[pl.ds(s * tok, tok)])
+            top += across(tall[origins[s], :, wide], gpre[pl.ds(s * tok, tok)])
         low = across(hid[:, thin], scaled[...])
         part[slot, :dq] = top.astype(BF16)
         part[slot, dq:] = low.astype(BF16)
@@ -367,8 +402,9 @@
     to_cross.start()
     partial(3, q)
 
-    for copy in backs:
-        copy.wait_recv()
+    for s in range(1, 4):
+        peer = (z + s) % 4
+        link(10 + s, back.at[s], rall.at[peer], "expert", peer, 53 + peer).wait_recv()
     total = jnp.zeros((tok, width), F32)
     for s in range(4):
         total += rall[s].astype(F32)
@@ -386,11 +422,12 @@
         def _(n=n):
             gext[pl.ds((n + 1) * tok, tok)] = jnp.zeros((tok, width), BF16)
 
-    for copy in gate_sums:
-        copy.wait_recv()
+    for s in range(1, 4):
+        peer = (z + s) % 4
+        link(33 + s, sums.at[s], sums_in.at[peer], "expert", peer, 57 + peer).wait_recv()
     gate_grads = jnp.zeros(ids.shape, F32)
     for s in range(4):
-        gate_grads += jnp.where(ids == (z + s) % 4, as_column(sums_in[s, 0:1]), 0.0)
+        gate_grads += jnp.where(ids == s, as_column(sums_in[s, 0:1]), 0.0)
     gg_ref[...] = jnp.where(slots_ref[...] < tok, gate_grads, 0.0).astype(BF16)
 
     quarter = taps // 4
@@ -479,8 +516,11 @@
         @pl.when(q >= n + 1)
         def _(n=n):
             halo_back[n].wait_send()
+    for d in range(3):
+        spread(37, gall, d, False)
+        spread(45, tall, d, False)
     for copy in (
-        weighs + gate_sums + cots + [w_sib, w_cross, w_far] + rows_out + backs + to_sib + [to_cross]
+        weighs + gate_sums + [w_sib, w_cross, w_far] + backs + to_sib + [to_cross]
         + gf_seq + gf_exp + gf_out + gf_last
     ):
         copy.wait_send()
@@ -515,7 +555,7 @@
             vm(4, taps // 16, width), vm(4, taps // 16, width),
             vm(4, 4, taps // 16, width),
             pltpu.VMEM((4, 8, tok), F32), pltpu.VMEM((4, 8, tok), F32), pltpu.VMEM((4, 8, tok), F32),
-            pltpu.SemaphoreType.DMA((37,)), pltpu.SemaphoreType.DMA((37,)),
+            pltpu.SemaphoreType.DMA((65,)), pltpu.SemaphoreType.DMA((65,)),
         ],
         compiler_params=pltpu.CompilerParams(
             collective_id=0, has_side_effects=True, vmem_limit_bytes=52 * 1024 * 1024

time: 132 us -> 119 us (0.902); the launches traced: 131 us -> 119 us
  Pallas kernels: 120 us -> 108 us
    pallas_call x1, Pallas kernels: 120 us -> 108 us  [dense_body(): pl.pallas_call(dense_kernel, out_shape=(jax.ShapeDtypeStruct((tok, width)...]
where the time goes in v3:
time: 119 us
  Pallas kernels  108 us (91%)
  local copies, waits for them, and re-layouts  10.2 us (9%)
    pallas_call x1, Pallas kernels, dense_body(): pl.pallas_call(dense_kernel, out_shape=(jax.ShapeDtypeStruct((tok, width)...  108 us
    unnamed x18, local copies, waits for them, and re-layouts  9.57 us

profile of v3, /device:TPU:1, one launch (start us, length us, event | category | flops | bytes accessed | tf_op | source)
XLA Modules:
  0.0 119.1 jit_solution(2810291028190424654)
XLA Ops:
  0.6 0.0 copy-start.3
  0.6 0.8 copy.19.gates_ref
  1.5 0.0 copy-done.3
  1.5 0.0 copy-start.4
  1.5 0.1 copy.20.ids_ref
  1.6 0.6 copy-done.4
  2.1 0.1 copy.21.slots_ref
  2.3 0.0 copy-start
  2.3 0.9 copy-done
  3.2 0.0 copy-start.1
  3.2 0.9 copy-done.1
  4.2 0.0 copy-start.2
  4.2 0.9 copy-done.2
  5.1 108.2 %shard_map.172 = (bf16[128,1024]{1,0:T(8,128)(2,1)S(1)}, bf16[128,4]{1,0:T(8,128)(2,1)S(1)}, f32[256,1024]{1,0:T(8,128)}, bf16[1,256,512]{2,1,0:T(8,128)(2,1)S(1...) custom-call(bf16[128,1024]{1,0:T(8,128)(2,1)S(1)} %copy-done, bf16[128,1024]{1,0:T(8,128)(2,1)S(1)} %copy-done.1, ...), custom_call_target="tpu_custom_call" | custom-call | tf_op jit(solution)/shard_map/pallas_call | solution.py:536
  113.4 0.7 copy.22
  114.0 0.7 copy.28
  114.7 2.3 %copy.29 = f32[256,1024]{1,0:T(8,128)} copy(f32[256,1024]{1,0:T(8,128)} %get-tuple-element.20) | data formatting | bytes 2097152
  117.0 0.7 copy.30
  117.7 0.7 copy.31
  118.4 0.7 copy.32
Async XLA Ops:
  0.6 0.8 copy-start.3
  1.5 0.7 copy-start.4
  2.3 0.9 copy-start
  3.2 0.9 copy-start.1
  4.2 0.9 copy-start.2

commit v4 on v3

--- a/solution.py
+++ b/solution.py
@@ -234,20 +234,6 @@
     for s in range(1, 4):
         pl.semaphore_signal(barrier, inc=1, device_id={"expert": (z + s) % 4}, device_id_type=MESH)
         pl.semaphore_signal(barrier, inc=1, device_id={"seq": (q + s) % 4}, device_id_type=MESH)
-    pl.semaphore_wait(barrier, 6)
-
-    halo = [
-        link(n, rows_ref, xext.at[pl.ds(reach_at - (n + 1) * tok, tok)], "seq", (q + n + 1) % 4)
-        for n in range(2)
-    ]
-    for n in range(2):
-        @pl.when(q + n + 1 < 4)
-        def _(n=n):
-            halo[n].start()
-
-        @pl.when(q < n + 1)
-        def _(n=n):
-            xext[pl.ds(reach_at - (n + 1) * tok, tok)] = jnp.zeros((tok, width), BF16)
 
     ids = ids_ref[...]
     held = jnp.where(slots_ref[...] < tok, gates_ref[...].astype(F32), 0.0)
@@ -266,20 +252,35 @@
         weigh[z, e:e + 1] = as_row(
             jnp.sum(jnp.where(ids == e, held, 0.0), axis=1, keepdims=True)
         )
-    weighs = [
-        link(30 + s, weigh.at[z], weigh.at[z], "expert", (z + s) % 4, 61 + z) for s in range(1, 4)
-    ]
-    for copy in weighs:
-        copy.start()
     gall[z] = cot_ref[...]
-    spread(37, gall, 0)
     wall[q, :dq, :ff] = wg_ref[0]
     wall[q, :dq, ff:] = wu_ref[0]
     wall[q, dq:] = wd_ref[0]
+    xext[pl.ds(reach_at, tok)] = rows_ref[...]
+    pl.semaphore_wait(barrier, 6)
+
+    halo = [
+        link(n, rows_ref, xext.at[pl.ds(reach_at - (n + 1) * tok, tok)], "seq", (q + n + 1) % 4)
+        for n in range(2)
+    ]
+    for n in range(2):
+        @pl.when(q + n + 1 < 4)
+        def _(n=n):
+            halo[n].start()
+
+        @pl.when(q < n + 1)
+        def _(n=n):
+            xext[pl.ds(reach_at - (n + 1) * tok, tok)] = jnp.zeros((tok, width), BF16)
+
+    weighs = [
+        link(30 + s, weigh.at[z], weigh.at[z], "expert", (z + s) % 4, 61 + z) for s in range(1, 4)
+    ]
+    for copy in weighs:
+        copy.start()
+    spread(37, gall, 0)
     w_sib = link(8, wall.at[q], wall.at[q], "seq", sib)
     w_cross = link(9, wall.at[q], wall.at[q], "seq", cross)
     w_sib.start()
-    xext[pl.ds(reach_at, tok)] = rows_ref[...]
 
     def cols(c):
         return pl.ds(pl.multiple_of(c * chunk, chunk), chunk)
@@ -506,7 +507,7 @@
         copy.wait_recv()
     for a in range(4):
         for b in range(4):
-            gf_ref[pl.ds((a * 4 + b) * piece, piece)] = gfull[a, b].astype(F32)
+            gf_ref[pl.ds((a * 4 + b) * piece, piece)] = gfull[a, b]
 
     for n in range(2):
         @pl.when(q + n + 1 < 4)
@@ -533,12 +534,12 @@
     size = taps + tok
     rows = w_gate.shape[1] + w_down.shape[1]
     vm = lambda *shape: pltpu.VMEM(shape, BF16)
-    return pl.pallas_call(
+    outs = pl.pallas_call(
         dense_kernel,
         out_shape=(
             jax.ShapeDtypeStruct((tok, width), BF16),
             jax.ShapeDtypeStruct(gates.shape, BF16),
-            jax.ShapeDtypeStruct((taps, width), F32),
+            jax.ShapeDtypeStruct((taps, width), BF16),
             jax.ShapeDtypeStruct(w_gate.shape, BF16),
             jax.ShapeDtypeStruct(w_up.shape, BF16),
             jax.ShapeDtypeStruct(w_down.shape, BF16),
@@ -564,6 +565,7 @@
         inputs, grad_out, gates, expert_ids, slot_index, w_gate, w_up, w_down, filter_taps,
         *[jnp.asarray(m) for m in transforms(size)],
     )
+    return outs[:2] + (outs[2].astype(F32),) + outs[3:]
 
 
 def body_of(mesh):

time: 119 us -> 119 us (level)
  local copies, waits for them, and re-layouts: 10.2 us -> 7.91 us
  other arithmetic: 0 us -> 2.13 us
    convert_element_type x0 -> x1, other arithmetic: none -> 2.13 us  [dense_body(): return outs[:2] + (outs[2].astype(F32),) + outs[3:]]
    unnamed x18, local copies, waits for them, and re-layouts: 9.57 us -> 7.91 us
where the time goes in v4:
time: 119 us; the launch traced here: 118 us
  Pallas kernels  108 us (91%)
  local copies, waits for them, and re-layouts  7.91 us (7%)
  other arithmetic  2.13 us (2%)
    pallas_call x1, Pallas kernels, dense_body(): pl.pallas_call(dense_kernel, out_shape=(jax.ShapeDtypeStruct((tok, width)...  108 us
    unnamed x18, local copies, waits for them, and re-layouts  7.91 us

profile of v4, /device:TPU:1, one launch (start us, length us, event | category | flops | bytes accessed | tf_op | source)
XLA Modules:
  0.0 118.4 jit_solution(16912466848721583247)
XLA Ops:
  0.6 0.0 copy-start.3
  0.6 0.8 copy.19.gates_ref
  1.5 0.0 copy-done.3
  1.5 0.0 copy-start.4
  1.5 0.1 copy.20.ids_ref
  1.6 0.6 copy-done.4
  2.1 0.1 copy.21.slots_ref
  2.3 0.0 copy-start
  2.3 0.9 copy-done
  3.2 0.0 copy-start.1
  3.2 0.9 copy-done.1
  4.2 0.0 copy-start.2
  4.2 0.9 copy-done.2
  5.1 107.7 %shard_map.172 = (bf16[128,1024]{1,0:T(8,128)(2,1)S(1)}, bf16[128,4]{1,0:T(8,128)(2,1)S(1)}, bf16[256,1024]{1,0:T(8,128)(2,1)}, bf16[1,256,512]{2,1,0:T(8,128)(2...) custom-call(bf16[128,1024]{1,0:T(8,128)(2,1)S(1)} %copy-done, ...), custom_call_target="tpu_custom_call" | custom-call | tf_op jit(solution)/shard_map/pallas_call | solution.py:537
  112.8 0.7 copy.22
  113.4 2.1 %convert_element_type.3 = f32[256,1024]{1,0:T(8,128)} convert(bf16[256,1024]{1,0:T(8,128)(2,1)} %get-tuple-element.14) | non-fusion elementwise | flops 262144 | bytes 1572864 | tf_op jit(solution)/shard_map/convert_element_type | solution.py:568
  115.6 0.7 copy.27
  116.3 0.7 copy.28
  117.0 0.7 copy.29
  117.7 0.7 copy.30
Async XLA Ops:
  0.6 0.8 copy-start.3
  1.5 0.7 copy-start.4
  2.3 0.9 copy-start
  3.2 0.9 copy-start.1
  4.2 0.9 copy-start.2
